TPU v7x, 32 devices: a whole 2x2x4 slice. The times are simulated.
32 devices in a mesh: gx: 8 (over z, core), gy: 4 (over y, x).
Axes of the slice: x: 2, y: 2, z: 4, core: 2. Of those that a mesh axis runs over, the one named last changes fastest.
Arguments:
- water_depth: float32 [1024, 1536], P('gx', 'gy'), may hold values from 0.3 to 3
- bed_level: float32 [1024, 1536], P('gx', 'gy'), may hold values from 0 to 2
- east_flow: float32 [1024, 1536], P('gx', 'gy'), may hold values from -4 to 4
- south_flow: float32 [1024, 1536], P('gx', 'gy'), may hold values from -4 to 4
- roughness_class: int32 [1024, 1536], P('gx', 'gy'), may hold values from 0 to 7
- wet_mask: int32 [1024, 1536], P('gx', 'gy'), may hold values 0 or 1
- soil_store: float32 [8, 1536, 128], P('gx', 'gy'), may hold values from 0.05 to 0.95
- rainfall: float32 [8, 1536, 128], P('gx', 'gy'), may hold values from 0 to 0.5
- tile_column: int32 [8, 1536, 1], P('gx', 'gy'), may hold values from 0 to 3; in each aligned block of 384 rows (0 to 383, 384 to 767, ..., all dimensions but the last counted through in order) at most 192 rows name the same one
- tile_block: int32 [8, 1536], P('gx', 'gy'), may hold values from 0 to 383
Outputs:
- new_depth: float32 [1024, 1536], P('gx', 'gy')
- new_east_flow: float32 [1024, 1536], P('gx', 'gy')
- new_south_flow: float32 [1024, 1536], P('gx', 'gy')
- new_soil: float32 [8, 1536, 128], P('gx', 'gy')
Inputs may be any that keep to these rules, and one draw needn't show every extreme that they name: `tile_column`: among the 384 land blocks of one device, at most 192 name the same tile column; in some device some tile column is named by exactly 192 of them. `tile_block`: several land blocks may name the same block of a tile; some blocks are named by none.
All inputs are finite; a program needn't handle non-finite values. No bound on the sum of `wet_mask` on one device may be relied on, other than what follows from the above.
Results may differ from a plain program's by a relative error of at most 0.00002.
Values sent between devices are 32-bit elements; how exact they have to be, the bound alone decides.
A program may use at most 64 MiB of HBM per device.

v0:
```python
import jax
import jax.numpy as jnp
from jax import lax
from jax.sharding import PartitionSpec as P

SUB = 4


GRAVITY = 9.81
TIME_STEP = 1.0
CELL_WIDTH = 30.0
DEPTH_FLOOR = 0.3
INFIL_RATE = 0.5
MANNING = (0.02, 0.03, 0.035, 0.045, 0.06, 0.08, 0.1, 0.15)


def padded_2(cells, sides, width):
    for axis, dim in sides:
        count = lax.axis_size(axis)
        ends = count - 1
        head = lax.slice_in_dim(cells, 0, width, axis=dim)
        tail = lax.slice_in_dim(cells, cells.shape[dim] - width, cells.shape[dim], axis=dim)
        cells = jnp.concatenate(
            [
                lax.ppermute(tail, axis, [(i, (i + 1) % count) for i in range(ends)]),
                cells,
                lax.ppermute(head, axis, [((i + 1) % count, i) for i in range(ends)]),
            ],
            axis=dim,
        )
    return cells


def roughness(roughness_class, wet_mask):
    friction = jnp.zeros(roughness_class.shape, jnp.float32)
    for class_index, coefficient in enumerate(MANNING):
        friction = jnp.where(roughness_class == class_index, coefficient * coefficient, friction)
    return jnp.where(wet_mask > 0, friction, -1.0)


def face_flow(
    upper_first, upper_second, base_first, base_second, fric_first, fric_second, previous
):
    flow_depth = jnp.maximum(upper_first, upper_second) - jnp.maximum(base_first, base_second)
    driving = (
        GRAVITY
        * TIME_STEP
        * jnp.maximum(flow_depth, 0.0)
        * (upper_second - upper_first)
        / CELL_WIDTH
    )
    mean_fric = 0.5 * (jnp.maximum(fric_first, 0.0) + jnp.maximum(fric_second, 0.0))
    damping = 1.0 + GRAVITY * TIME_STEP * mean_fric * jnp.abs(previous) / jnp.maximum(
        flow_depth, DEPTH_FLOOR
    ) ** (7.0 / 3.0)
    is_open = (fric_first > 0) & (fric_second > 0)
    return jnp.where(is_open, (previous - driving) / damping, 0.0)


def advance(height, eastward, southward, bottom, friction):
    surface = bottom + height
    new_east = face_flow(
        surface[1:-1, :-1],
        surface[1:-1, 1:],
        bottom[1:-1, :-1],
        bottom[1:-1, 1:],
        friction[1:-1, :-1],
        friction[1:-1, 1:],
        eastward[1:-1, :-1],
    )
    new_south = face_flow(
        surface[:-1, 1:-1],
        surface[1:, 1:-1],
        bottom[:-1, 1:-1],
        bottom[1:, 1:-1],
        friction[:-1, 1:-1],
        friction[1:, 1:-1],
        southward[:-1, 1:-1],
    )
    change = new_east[:, :-1] - new_east[:, 1:] + new_south[:-1, :] - new_south[1:, :]
    return (height[1:-1, 1:-1] + TIME_STEP / CELL_WIDTH * change, new_east[:, 1:], new_south[1:, :])


def local(
    water_depth,
    bed_level,
    east_flow,
    south_flow,
    roughness_class,
    wet_mask,
    soil_store,
    rainfall,
    tile_column,
    tile_block,
):
    tile_rows, tile_columns = water_depth.shape
    land_rows = tile_rows * tile_columns // 128
    runoff = rainfall[0] * soil_store[0] * soil_store[0]
    column = tile_column[0, :, 0]
    owner_block = tile_block[0]
    target = column * land_rows + owner_block
    count = land_rows * lax.axis_size("gy")
    offset = target
    inside = (offset >= 0) & (offset < count)
    segment = jnp.where(inside, offset, count)
    inflow = lax.psum_scatter(
        jax.ops.segment_sum(runoff, segment, num_segments=count + 1)[:count],
        "gy",
        scatter_dimension=0,
        tiled=True,
    )
    surface = water_depth + inflow.reshape(tile_rows, tile_columns)
    friction = roughness(roughness_class, wet_mask)
    padded = padded_2(
        jnp.stack([surface, east_flow, south_flow, bed_level, friction]),
        (("gx", 1), ("gy", 2)),
        SUB,
    )
    fields = (padded[0], padded[1], padded[2])
    for substep in range(SUB):
        extent_rows = tile_rows + 2 * (SUB - substep)
        extent_columns = tile_columns + 2 * (SUB - substep)
        bottom = padded[3, substep : substep + extent_rows, substep : substep + extent_columns]
        local_friction = padded[
            4, substep : substep + extent_rows, substep : substep + extent_columns
        ]
        fields = advance(fields[0], fields[1], fields[2], bottom, local_friction)
    new_depth, new_east, new_south = fields
    level_blocks = new_depth.reshape(land_rows, 128)
    piece = lax.all_gather(level_blocks, "gy", axis=0, tiled=True)
    offset = target
    inside = (offset >= 0) & (offset < piece.shape[0])
    chosen = piece[jnp.clip(offset, 0, piece.shape[0] - 1)]
    levels = jnp.where(inside[:, None], chosen, 0.0)
    infiltration = INFIL_RATE * (1.0 - soil_store[0]) * (1.0 - jnp.exp(-levels))
    new_soil = soil_store[0] + rainfall[0] - runoff + infiltration
    return (new_depth, new_east, new_south, new_soil[None])


def solution(mesh):
    in_specs = (
        P("gx", "gy"),
        P("gx", "gy"),
        P("gx", "gy"),
        P("gx", "gy"),
        P("gx", "gy"),
        P("gx", "gy"),
        P("gx", "gy", None),
        P("gx", "gy", None),
        P("gx", "gy", None),
        P("gx", "gy"),
    )
    out_specs = (P("gx", "gy"), P("gx", "gy"), P("gx", "gy"), P("gx", "gy", None))
    return jax.shard_map(local, mesh=mesh, in_specs=in_specs, out_specs=out_specs, check_vma=False)
```

profile of v0, /device:TPU:1, one launch (start us, length us, event | category | flops | bytes accessed | tf_op | source)
XLA Modules:
  0.0 96.4 jit_solution(15074529836560721229)
XLA Ops:
  7.2 0.7 fusion.28
  7.9 2.5 %scatter_custom_fusion = f32[1537,128]{1,0:T(8,128)S(1)} fusion(s32[384]{0:T(512)S(1)} %get-tuple-element.5, f32[]{:T(128)} %constant.28.clone.1, f32[1,384,128]{2,1,0:T(8,128)} %param.16, f32[1,384,128]{2,1,0:T(8,128)} %param.17), kind=kCustom, calls=%fused_computation.3 | custom fusion | flops 147456 | bytes 1180164 | tf_op jit(solution)/shard_map/scatter-add | solution.py:107
  10.5 0.9 slice.384
  11.5 28.1 %reduce-scatter.2.cloned.1.call-done = f32[384,128]{1,0:T(8,128)} async-done(((f32[1536,128]{1,0:T(8,128)}), f32[384,128]{1,0:T(8,128)}) %reduce-scatter.2.cloned.1.call-update) | async-done | bytes 196624 | tf_op jit(solution)/shard_map/reduce_scatter | solution.py:106
  39.6 1.0 %reshape.111 = f32[128,384]{1,0:T(8,128)S(1)} reshape(f32[384,128]{1,0:T(8,128)} %reduce-scatter.2.cloned.1.call-done) | data formatting | bytes 393216 | tf_op jit(solution)/shard_map/reshape | solution.py:112
  40.9 3.9 %collective-permute-start = (f32[5,4,384]{2,1,0:T(4,128)S(1)}, f32[5,4,384]{2,1,0:T(4,128)S(1)}, u32[]{:S(2)}, u32[]{:S(2)}) collective-permute-start(f32[5,4,384]{2,1,0:T(4,128)S(1)} %get-tuple-element.28), channel_id=1, source_target_pairs={{0,4},{4,8},{8,12},{12,16},{16,20},{20,24},{24,28},{1,5},{5,9},{9,... | collective-permute-start | bytes 92168 | tf_op jit(solution)/shard_map/ppermute | solution.py:25
  44.8 1.9 %collective-permute-start.1 = (f32[5,4,384]{2,1,0:T(4,128)S(1)}, f32[5,4,384]{2,1,0:T(4,128)S(1)}, u32[]{:S(2)}, u32[]{:S(2)}) collective-permute-start(f32[5,4,384]{2,1,0:T(4,128)S(1)} %get-tuple-element.29), channel_id=1, source_target_pairs={{4,0},{8,4},{12,8},{16,12},{20,16},{24,20},{28,24},{5,1},{9,5},{13... | collective-permute-start | bytes 92168 | tf_op jit(solution)/shard_map/ppermute | solution.py:27
  46.8 3.3 %collective-permute-done.1 = f32[5,4,384]{2,1,0:T(4,128)S(1)} collective-permute-done((f32[5,4,384]{2,1,0:T(4,128)S(1)}, f32[5,4,384]{2,1,0:T(4,128)S(1)}, u32[]{:S(2)}, u32[]{:S(2)}) %collective-permute-start.1) | collective-permute-done | bytes 30752 | tf_op jit(solution)/shard_map/ppermute | solution.py:27
  50.0 0.2 pad_maximum_fusion.3
  50.2 3.1 %collective-permute-start.2 = (f32[5,136,4]{2,1,0:T(8,128)S(1)}, f32[5,136,4]{2,1,0:T(8,128)S(1)}, u32[]{:S(2)}, u32[]{:S(2)}) collective-permute-start(f32[5,136,4]{2,1,0:T(8,128)S(1)} %get-tuple-element.26), channel_id=1, source_target_pairs={{0,1},{1,2},{2,3},{4,5},{5,6},{6,7},{8,9},{9,10},{10,11},{12,13},{... | collective-permute-start | bytes 32648 | tf_op jit(solution)/shard_map/ppermute | solution.py:25
  53.3 1.3 %collective-permute-start.3 = (f32[5,136,4]{2,1,0:T(8,128)S(1)}, f32[5,136,4]{2,1,0:T(8,128)S(1)}, u32[]{:S(2)}, u32[]{:S(2)}) collective-permute-start(f32[5,136,4]{2,1,0:T(8,128)S(1)} %get-tuple-element.27), channel_id=1, source_target_pairs={{1,0},{2,1},{3,2},{5,4},{6,5},{7,6},{9,8},{10,9},{11,10},{13,12},{... | collective-permute-start | bytes 32648 | tf_op jit(solution)/shard_map/ppermute | solution.py:27
  54.6 5.0 %collective-permute-done.2 = f32[5,136,4]{2,1,0:T(8,128)S(1)} collective-permute-done((f32[5,136,4]{2,1,0:T(8,128)S(1)}, f32[5,136,4]{2,1,0:T(8,128)S(1)}, u32[]{:S(2)}, u32[]{:S(2)}) %collective-permute-start.2) | collective-permute-done | bytes 10912 | tf_op jit(solution)/shard_map/ppermute | solution.py:25
  59.6 9.1 %collective-permute-done.3 = f32[5,136,4]{2,1,0:T(8,128)S(1)} collective-permute-done((f32[5,136,4]{2,1,0:T(8,128)S(1)}, f32[5,136,4]{2,1,0:T(8,128)S(1)}, u32[]{:S(2)}, u32[]{:S(2)}) %collective-permute-start.3) | collective-permute-done | bytes 10912 | tf_op jit(solution)/shard_map/ppermute | solution.py:27
  68.7 0.6 pad_maximum_fusion
  69.5 0.2 slice_bitcast_fusion.5
  69.7 0.6 divide_select_fusion.5
  70.3 0.6 divide_select_fusion.4
  70.9 0.3 fusion.30
  71.2 0.6 divide_select_fusion.3
  71.8 0.6 divide_select_fusion.2
  72.5 0.2 slice_bitcast_fusion.3
  72.7 0.3 fusion.31
  73.0 0.6 divide_select_fusion.1
  73.6 0.6 divide_select_fusion
  74.2 0.2 slice_bitcast_fusion.1
  74.5 0.3 fusion.32
  74.8 0.6 divide_select_fusion.6
  75.3 0.5 divide_select_fusion.7
  75.8 0.8 fusion.20
  76.7 10.8 %all_gather.3 = f32[1536,128]{1,0:T(8,128)S(1)} all-gather(f32[384,128]{1,0:T(8,128)S(1)} %reshape.112), channel_id=1, replica_groups=mesh['gx'=8,'gy'=4] {'gy'}, dimensions={0}, use_global_device_ids=true | all-gather | bytes 983040 | tf_op jit(solution)/shard_map/all_gather | solution.py:130
  87.6 1.1 %gather_fusion = f32[384,128]{1,0:T(8,128)S(1)} fusion(f32[1536,128]{1,0:T(8,128)S(1)} %all_gather.3, s32[1024]{0:T(1024)S(1)} %pad_clamp_fusion), kind=kCustom, calls=%fused_computation | custom fusion | bytes 394752 | tf_op jit(solution)/shard_map/gather | solution.py:133
  88.7 0.8 fusion.17
  (38 shorter events, 0.6 us)
Async XLA Ops:
  7.2 32.5 %reduce-scatter.2.cloned.1.call-start = ((), (), s32[]{:S(2)}) async-start(), calls=%async_computation.1 | async-start | bytes 983040 | tf_op jit(solution)/shard_map/reduce_scatter | solution.py:106
  10.4 1.0 %copy-start.10 = (s32[1,384]{1,0:T(1,128)S(1)}, s32[1,384]{1,0:T(1,128)}, u32[]{:S(2)}) copy-start(s32[1,384]{1,0:T(1,128)} %param.19) | copy-start | bytes 4612
  10.4 1.0 %copy-start.9 = (s32[1,384,1]{1,2,0:T(1,128)S(1)}, s32[1,384,1]{1,2,0:T(1,128)}, u32[]{:S(2)}) copy-start(s32[1,384,1]{1,2,0:T(1,128)} %param.18) | copy-start | bytes 4612
  10.5 30.1 %copy-start.6 = (f32[128,384]{1,0:T(8,128)S(1)}, f32[128,384]{1,0:T(8,128)}, u32[]{:S(2)}) copy-start(f32[128,384]{1,0:T(8,128)} %param.10) | copy-start | bytes 589828
  10.5 30.2 %copy-start.3 = (f32[128,384]{1,0:T(8,128)S(1)}, f32[128,384]{1,0:T(8,128)}, u32[]{:S(2)}) copy-start(f32[128,384]{1,0:T(8,128)} %param.12) | copy-start | bytes 589828
  11.4 29.2 %copy-start.4 = (f32[128,384]{1,0:T(8,128)S(1)}, f32[128,384]{1,0:T(8,128)}, u32[]{:S(2)}) copy-start(f32[128,384]{1,0:T(8,128)} %param.13) | copy-start | bytes 589828
  11.4 29.3 %copy-start.5 = (f32[128,384]{1,0:T(8,128)S(1)}, f32[128,384]{1,0:T(8,128)}, u32[]{:S(2)}) copy-start(f32[128,384]{1,0:T(8,128)} %param.11) | copy-start | bytes 589828
  11.4 29.3 %copy-start.7 = (s32[128,384]{1,0:T(8,128)S(1)}, s32[128,384]{1,0:T(8,128)}, u32[]{:S(2)}) copy-start(s32[128,384]{1,0:T(8,128)} %param.14) | copy-start | bytes 589828
  11.4 29.3 %copy-start.8 = (s32[128,384]{1,0:T(8,128)S(1)}, s32[128,384]{1,0:T(8,128)}, u32[]{:S(2)}) copy-start(s32[128,384]{1,0:T(8,128)} %param.15) | copy-start | bytes 589828
  40.9 5.8 %collective-permute-start = (f32[5,4,384]{2,1,0:T(4,128)S(1)}, f32[5,4,384]{2,1,0:T(4,128)S(1)}, u32[]{:S(2)}, u32[]{:S(2)}) collective-permute-start(f32[5,4,384]{2,1,0:T(4,128)S(1)} %get-tuple-element.28), channel_id=1, source_target_pairs={{0,4},{4,8},{8,12},{12,16},{16,20},{20,24},{24,28},{1,5},{5,9},{9,... | collective-permute-start | bytes 92168 | tf_op jit(solution)/shard_map/ppermute | solution.py:25
  44.8 5.2 %collective-permute-start.1 = (f32[5,4,384]{2,1,0:T(4,128)S(1)}, f32[5,4,384]{2,1,0:T(4,128)S(1)}, u32[]{:S(2)}, u32[]{:S(2)}) collective-permute-start(f32[5,4,384]{2,1,0:T(4,128)S(1)} %get-tuple-element.29), channel_id=1, source_target_pairs={{4,0},{8,4},{12,8},{16,12},{20,16},{24,20},{28,24},{5,1},{9,5},{13... | collective-permute-start | bytes 92168 | tf_op jit(solution)/shard_map/ppermute | solution.py:27
  50.2 9.4 %collective-permute-start.2 = (f32[5,136,4]{2,1,0:T(8,128)S(1)}, f32[5,136,4]{2,1,0:T(8,128)S(1)}, u32[]{:S(2)}, u32[]{:S(2)}) collective-permute-start(f32[5,136,4]{2,1,0:T(8,128)S(1)} %get-tuple-element.26), channel_id=1, source_target_pairs={{0,1},{1,2},{2,3},{4,5},{5,6},{6,7},{8,9},{9,10},{10,11},{12,13},{... | collective-permute-start | bytes 32648 | tf_op jit(solution)/shard_map/ppermute | solution.py:25
  53.3 15.4 %collective-permute-start.3 = (f32[5,136,4]{2,1,0:T(8,128)S(1)}, f32[5,136,4]{2,1,0:T(8,128)S(1)}, u32[]{:S(2)}, u32[]{:S(2)}) collective-permute-start(f32[5,136,4]{2,1,0:T(8,128)S(1)} %get-tuple-element.27), channel_id=1, source_target_pairs={{1,0},{2,1},{3,2},{5,4},{6,5},{7,6},{9,8},{10,9},{11,10},{13,12},{... | collective-permute-start | bytes 32648 | tf_op jit(solution)/shard_map/ppermute | solution.py:27
  76.7 12.0 %copy-start = (f32[128,384]{1,0:T(8,128)}, f32[128,384]{1,0:T(8,128)S(1)}, u32[]{:S(2)}) copy-start(f32[128,384]{1,0:T(8,128)S(1)} %get-tuple-element.6) | copy-start | bytes 589828
  76.7 12.0 %copy-start.1 = (f32[1,384,128]{2,1,0:T(8,128)S(1)}, f32[1,384,128]{2,1,0:T(8,128)}, u32[]{:S(2)}) copy-start(f32[1,384,128]{2,1,0:T(8,128)} %param.16) | copy-start | bytes 589828
  76.7 12.0 %copy-start.2 = (f32[1,384,128]{2,1,0:T(8,128)S(1)}, f32[1,384,128]{2,1,0:T(8,128)}, u32[]{:S(2)}) copy-start(f32[1,384,128]{2,1,0:T(8,128)} %param.17) | copy-start | bytes 589828
Sparse Core Ops, SparseCore 0:
  11.6 27.9 reduce-scatter.1
where the time goes:
time: 97.4 us; the launch traced here: 96.4 us
  waiting for transfers between devices  45.4 us (47%)
  between operations  14.4 us (15%)
  other arithmetic  11.5 us (12%)
  blocking collectives  10.8 us (11%)
  starting transfers between devices  10.2 us (10%)
  local copies, waits for them, and re-layouts  3.97 us (4%)
    reduce_scatter x1, waiting for transfers between devices, local(): lax.psum_scatter(jax.ops.segment_sum(runoff, segment, num_segments=count...  28.1 us
    ppermute x2, waiting for transfers between devices, padded_2(): lax.ppermute(head, axis, [((i + 1) % count, i) for i in range(ends)])  12.3 us
    all_gather x1, blocking collectives, local(): piece = lax.all_gather(level_blocks, 'gy', axis=0, tiled=True)  10.8 us
    ppermute x2, starting transfers between devices, padded_2(): lax.ppermute(tail, axis, [(i, (i + 1) % count) for i in range(ends)])  6.99 us
    ppermute x2, waiting for transfers between devices, padded_2(): lax.ppermute(tail, axis, [(i, (i + 1) % count) for i in range(ends)])  4.98 us
    select_n x8, other arithmetic, face_flow(): return jnp.where(is_open, (previous - driving) / damping, 0.0)  4.73 us
    ppermute x2, starting transfers between devices, padded_2(): lax.ppermute(head, axis, [((i + 1) % count, i) for i in range(ends)])  3.21 us
    scatter-add x1, other arithmetic, local(): jax.ops.segment_sum(runoff, segment, num_segments=count + 1)[:count]  2.49 us
  transfers between devices with their start and end apart: 5, of which 4 were waited for; matrix products, arithmetic and copies ran while one was open for 0% of the time, Pallas kernels for 0%

commit v1 on v0

v1 whole, which is shorter than its diff:
```python
import functools

import jax
import jax.numpy as jnp
from jax import lax
from jax.experimental import pallas as pl
from jax.experimental.pallas import tpu as pltpu
from jax.sharding import PartitionSpec as P

SUB = 4
GRAVITY = 9.81
TIME_STEP = 1.0
CELL_WIDTH = 30.0
DEPTH_FLOOR = 0.3
INFIL_RATE = 0.5
MANNING = (0.02, 0.03, 0.035, 0.045, 0.06, 0.08, 0.1, 0.15)
LANES = 128
EDGE = 8
MESH = pl.DeviceIdType.MESH
AROUND = ((-1, -1), (-1, 0), (-1, 1), (0, -1), (0, 1), (1, -1), (1, 0), (1, 1))
NW, N, NE, W, E, SW, S, SE = range(8)


def split3(x):
    a = x.astype(jnp.bfloat16)
    rest = x - a.astype(jnp.float32)
    b = rest.astype(jnp.bfloat16)
    c = (rest - b.astype(jnp.float32)).astype(jnp.bfloat16)
    return jnp.concatenate([a, b, c], axis=1)


def pick(mask, x):
    y = jnp.dot(mask, split3(x), preferred_element_type=jnp.float32)
    return y[:, :LANES] + y[:, LANES : 2 * LANES] + y[:, 2 * LANES :]


def east_of(x):
    return pltpu.roll(x, x.shape[1] - 1, 1)


def south_of(x):
    return pltpu.roll(x, x.shape[0] - 1, 0)


def face(eta, eta_next, base, coef, q):
    depth = jnp.maximum(eta, eta_next) - base
    driving = (GRAVITY * TIME_STEP / CELL_WIDTH) * jnp.maximum(depth, 0.0) * (eta_next - eta)
    power = jnp.exp2(jnp.log2(jnp.maximum(depth, DEPTH_FLOOR)) * (-7.0 / 3.0))
    damping = 1.0 + coef * jnp.abs(q) * power
    return jnp.where(coef > 0.0, (q - driving) / damping, 0.0)


def kernel(
    nx, ny, cap,
    depth_in, bed_in, east_in, south_in, rough_in, wet_in, soil_in, rain_in, col_in, blk_in,
    depth_out, east_out, south_out, soil_out,
    h, bed, qe, qs, fric, rough, wet, soil, rain, col, blk, newsoil,
    base_e, base_s, coef_e, coef_s,
    give, take, give_idx, take_idx, give_lev, take_lev,
    st_rows, st_cols, st_in_rows, st_in_cols, st_in_corner,
    h_rows, h_cols, h_in_rows, h_in_cols, h_in_corner,
    place, place_t, where_to, where_to_t,
    in_sem, out_sem, give_s, give_r, idx_s, idx_r, lev_s, lev_r, st_s, st_r, hs_s, hs_r,
):
    gx, gy = lax.axis_index("gx"), lax.axis_index("gy")
    tr, tc = rough.shape
    land = soil.shape[0]
    chunks = tc // LANES

    inner = (pl.ds(0, tr), pl.ds(0, tc))
    loads = [
        pltpu.make_async_copy(src, dst, in_sem.at[i])
        for i, (src, dst) in enumerate(
            [
                (col_in, col), (blk_in, blk), (soil_in, soil), (rain_in, rain),
                (rough_in, rough), (wet_in, wet), (bed_in, bed.at[inner]),
                (east_in, qe.at[inner]), (south_in, qs.at[inner]), (depth_in, h.at[inner]),
            ]
        )
    ]
    for c in loads:
        c.start()

    def there(k):
        dx, dy = AROUND[k]
        x, y = gx + dx, gy + dy
        return (x >= 0) & (x < nx) & (y >= 0) & (y < ny)

    barrier = pltpu.get_barrier_semaphore()
    for k in range(1, ny):
        pl.semaphore_signal(
            barrier, inc=1, device_id=(gx, lax.rem(gy + k, ny)), device_id_type=MESH
        )
    total = ny - 1
    for k in (NW, N, NE, SW, S, SE):
        dx, dy = AROUND[k]

        @pl.when(there(k))
        def _(dx=dx, dy=dy):
            pl.semaphore_signal(barrier, inc=1, device_id=(gx + dx, gy + dy), device_id_type=MESH)

        total = total + there(k).astype(jnp.int32)

    for k, ref in ((N, (st_in_rows, h_in_rows)), (S, (st_in_rows, h_in_rows))):
        @pl.when(jnp.logical_not(there(k)))
        def _(k=k, ref=ref):
            for r in ref:
                r[int(k == S)] = jnp.zeros(r.shape[1:], r.dtype)
    for k, ref in ((W, (st_in_cols, h_in_cols)), (E, (st_in_cols, h_in_cols))):
        @pl.when(jnp.logical_not(there(k)))
        def _(k=k, ref=ref):
            for r in ref:
                r[int(k == E)] = jnp.zeros(r.shape[1:], r.dtype)
    for n, k in enumerate((NW, NE, SW, SE)):
        @pl.when(jnp.logical_not(there(k)))
        def _(n=n):
            for r in (st_in_corner, h_in_corner):
                r[n] = jnp.zeros(r.shape[1:], r.dtype)

    loads[0].wait()
    loads[1].wait()
    column = col[...]
    groups = max(EDGE, ny)
    is_col = lax.broadcasted_iota(jnp.int32, (groups, land), 0) == column
    before = lax.broadcasted_iota(jnp.int32, (land, land), 0) < lax.broadcasted_iota(
        jnp.int32, (land, land), 1
    )
    rank = jnp.dot(
        is_col.astype(jnp.float32).astype(jnp.bfloat16),
        before.astype(jnp.float32).astype(jnp.bfloat16),
        preferred_element_type=jnp.float32,
    )
    rank = jnp.sum(jnp.where(is_col, rank, 0.0), axis=0, keepdims=True)
    slot = column.astype(jnp.float32) * cap + rank
    slots = ny * cap
    hit = lax.broadcasted_iota(jnp.int32, (slots, land), 0).astype(jnp.float32) == slot
    hit = hit.astype(jnp.float32)
    place[...] = hit.astype(jnp.bfloat16)

    block = blk[...].astype(jnp.float32)
    row = jnp.floor((block + 0.5) * (1.0 / chunks))
    chunk = block - row * chunks
    line = lax.broadcasted_iota(jnp.int32, (EDGE, land), 0)
    code = jnp.where(line == 0, row + 1.0, jnp.where(line == 1, chunk, 0.0))
    code = lax.dot_general(
        code.astype(jnp.bfloat16), place[...], (((1,), (1,)), ((), ())),
        preferred_element_type=jnp.float32,
    )
    owner = jnp.broadcast_to(code[1:2] * tr + code[0:1] - 1.0, (EDGE, slots))
    for d in range(ny):
        give_idx[d] = owner[:, d * cap : (d + 1) * cap]

    loads[2].wait()
    loads[3].wait()
    runoff = rain[...] * soil[...] * soil[...]
    packed = pick(place[...], runoff)
    for d in range(ny):
        give[d] = packed[d * cap : (d + 1) * cap]

    pl.semaphore_wait(barrier, total)

    def to_all(src, dst, ss, rs):
        out = []
        for k in range(1, ny):
            peer = lax.rem(gy + k, ny)
            out.append(
                pltpu.make_async_remote_copy(
                    src_ref=src.at[peer], dst_ref=dst.at[gy], send_sem=ss.at[k - 1],
                    recv_sem=rs.at[k - 1], device_id=(gx, peer), device_id_type=MESH,
                )
            )
        for c in out:
            c.start()
        return out

    def from_all(dst, src, ss, rs):
        for k in range(1, ny):
            peer = lax.rem(gy + ny - k, ny)
            pltpu.make_async_remote_copy(
                src_ref=src.at[peer], dst_ref=dst.at[peer], send_sem=ss.at[k - 1],
                recv_sem=rs.at[k - 1], device_id=(gx, peer), device_id_type=MESH,
            ).wait_recv()

    sent = to_all(give_idx, take_idx, idx_s, idx_r)
    sent += to_all(give, take, give_s, give_r)
    take_idx[pl.ds(gy, 1)] = give_idx[pl.ds(gy, 1)]
    take[pl.ds(gy, 1)] = give[pl.ds(gy, 1)]

    for i in range(4, 9):
        loads[i].wait()
    kind = rough[...]
    f = jnp.zeros((tr, tc), jnp.float32)
    for i, coefficient in enumerate(MANNING):
        f = jnp.where(kind == i, coefficient * coefficient, f)
    fric[inner] = jnp.where(wet[...] > 0, f, -1.0)
    lane_low = lax.broadcasted_iota(jnp.int32, (tr, LANES), 1) < LANES // 2

    def stage(fields, rows, cols):
        for i, ref in enumerate(fields):
            rows[0, i] = ref[0:EDGE, 0:tc]
            rows[1, i] = ref[tr - EDGE : tr, 0:tc]
            ends = jnp.where(lane_low, ref[0:tr, 0:LANES], ref[0:tr, tc - LANES : tc]).T
            cols[0, i] = ends[0:EDGE]
            cols[1, i] = ends[LANES - EDGE :]

    def edges(rows, cols, in_rows, in_cols, in_corner, ss, rs):
        first, last = pl.ds(0, LANES), pl.ds(tc - LANES, LANES)

        def piece(k):
            dx, dy = AROUND[k]
            if dy == 0:
                return rows.at[int(dx > 0)], in_rows.at[int(dx < 0)]
            if dx == 0:
                return cols.at[int(dy > 0)], in_cols.at[int(dy < 0)]
            side = last if dy > 0 else first
            corner = {NW: 3, NE: 2, SW: 1, SE: 0}[k]
            return rows.at[int(dx > 0), :, :, side], in_corner.at[corner]

        def copy(k):
            dx, dy = AROUND[k]
            src, dst = piece(k)
            return pltpu.make_async_remote_copy(
                src_ref=src, dst_ref=dst, send_sem=ss.at[k], recv_sem=rs.at[7 - k],
                device_id=(gx + dx, gy + dy), device_id_type=MESH,
            )

        def start():
            for k in (NW, NE, SW, SE, W, E, N, S):
                @pl.when(there(k))
                def _(k=k):
                    copy(k).start()

        def wait_recv():
            for k in range(8):
                @pl.when(there(k))
                def _(k=k):
                    copy(7 - k).wait_recv()

        def wait_send():
            for k in range(8):
                @pl.when(there(k))
                def _(k=k):
                    copy(k).wait_send()

        return start, wait_recv, wait_send

    sub_low = lax.broadcasted_iota(jnp.int32, (EDGE, 1), 0) < EDGE // 2

    def unstage(fields, in_rows, in_cols, in_corner):
        for i, ref in enumerate(fields):
            ref[tr : tr + EDGE, 0:tc] = jnp.where(sub_low, in_rows[1, i], in_rows[0, i])
            side = jnp.concatenate(
                [in_cols[1, i], jnp.zeros((LANES - 2 * EDGE, tr), jnp.float32), in_cols[0, i]],
                axis=0,
            )
            ref[0:tr, tc : tc + LANES] = side.T
            ref[tr : tr + EDGE, tc : tc + LANES] = jnp.where(
                lane_low[:EDGE],
                jnp.where(sub_low, in_corner[3, i], in_corner[1, i]),
                jnp.where(sub_low, in_corner[2, i], in_corner[0, i]),
            )

    fixed = (bed, fric, qe, qs)
    stage(fixed, st_rows, st_cols)
    st_start, st_wait, st_done = edges(
        st_rows, st_cols, st_in_rows, st_in_cols, st_in_corner, st_s, st_r
    )
    st_start()

    place_t[...] = hit.T.astype(jnp.bfloat16)

    from_all(take_idx, give_idx, idx_s, idx_r)
    ids = jnp.concatenate([take_idx[d] for d in range(ny)], axis=1)[0:1]
    target = lax.broadcasted_iota(jnp.int32, (land, slots), 0).astype(jnp.float32) == ids
    target = target.astype(jnp.float32)
    where_to[...] = target.astype(jnp.bfloat16)
    where_to_t[...] = target.T.astype(jnp.bfloat16)

    st_wait()
    unstage(fixed, st_in_rows, st_in_cols, st_in_corner)
    b, fr = bed[...], fric[...]
    b_e, f_e, b_s, f_s = east_of(b), east_of(fr), south_of(b), south_of(fr)
    half = 0.5 * GRAVITY * TIME_STEP
    base_e[...] = jnp.maximum(b, b_e)
    base_s[...] = jnp.maximum(b, b_s)
    coef_e[...] = jnp.where((fr > 0.0) & (f_e > 0.0), half * (fr + f_e), -1.0)
    coef_s[...] = jnp.where((fr > 0.0) & (f_s > 0.0), half * (fr + f_s), -1.0)

    loads[9].wait()
    from_all(take, give, give_s, give_r)
    inflow = pick(where_to[...], take[...].reshape(slots, LANES))
    for c in range(chunks):
        at = (pl.ds(0, tr), pl.ds(c * LANES, LANES))
        h[at] = h[at] + inflow[c * tr : (c + 1) * tr]

    stage((h,), h_rows, h_cols)
    h_start, h_wait, h_done = edges(
        h_rows, h_cols, h_in_rows, h_in_cols, h_in_corner, hs_s, hs_r
    )
    h_start()
    h_wait()
    unstage((h,), h_in_rows, h_in_cols, h_in_corner)

    for step in range(SUB):
        eta = h[...] + bed[...]
        e = face(eta, east_of(eta), base_e[...], coef_e[...], qe[...])
        s = face(eta, south_of(eta), base_s[...], coef_s[...], qs[...])
        qe[...] = e
        qs[...] = s
        h[...] = h[...] + (TIME_STEP / CELL_WIDTH) * (
            pltpu.roll(e, 1, 1) - e + pltpu.roll(s, 1, 0) - s
        )

    stores = [
        pltpu.make_async_copy(src.at[inner], dst, out_sem.at[i])
        for i, (src, dst) in enumerate([(h, depth_out), (qe, east_out), (qs, south_out)])
    ]
    for c in stores:
        c.start()
    blocks = jnp.concatenate(
        [h[0:tr, c * LANES : (c + 1) * LANES] for c in range(chunks)], axis=0
    )
    levels = pick(where_to_t[...], blocks)
    for d in range(ny):
        give_lev[d] = levels[d * cap : (d + 1) * cap]
    sent += to_all(give_lev, take_lev, lev_s, lev_r)
    take_lev[pl.ds(gy, 1)] = give_lev[pl.ds(gy, 1)]
    from_all(take_lev, give_lev, lev_s, lev_r)
    mine = pick(place_t[...], take_lev[...].reshape(slots, LANES))
    store = soil[...]
    runoff = rain[...] * store * store
    newsoil[...] = (
        store + rain[...] - runoff + INFIL_RATE * (1.0 - store) * (1.0 - jnp.exp(-mine))
    )
    last = pltpu.make_async_copy(newsoil, soil_out, out_sem.at[3])
    last.start()
    for c in sent:
        c.wait_send()
    st_done()
    h_done()
    for c in stores:
        c.wait()
    last.wait()


def local(depth, bed, east, south, rough, wet, soil, rain, column, block):
    nx, ny = lax.axis_size("gx"), lax.axis_size("gy")
    tr, tc = depth.shape
    land = soil.shape[1]
    cap = 2 * land // ny
    slots = ny * cap
    grid = (tr + EDGE, tc + LANES)
    f32, bf16, i32 = jnp.float32, jnp.bfloat16, jnp.int32
    v = pltpu.VMEM
    dma = pltpu.SemaphoreType.DMA
    peers = max(1, ny - 1)

    def edge_bufs(k):
        return [
            v((2, k, EDGE, tc), f32), v((2, k, EDGE, tr), f32),
            v((2, k, EDGE, tc), f32), v((2, k, EDGE, tr), f32), v((4, k, EDGE, LANES), f32),
        ]

    any_ = pl.BlockSpec(memory_space=pl.ANY)
    shape = jax.ShapeDtypeStruct
    out = pl.pallas_call(
        functools.partial(kernel, nx, ny, cap),
        out_shape=[shape((tr, tc), f32)] * 3 + [shape((land, LANES), f32)],
        in_specs=[any_] * 10,
        out_specs=[any_] * 4,
        scratch_shapes=[v(grid, f32)] * 5
        + [v((tr, tc), i32)] * 2
        + [v((land, LANES), f32)] * 2
        + [v((1, land), i32)] * 2
        + [v((land, LANES), f32)]
        + [v(grid, f32)] * 4
        + [v((ny, cap, LANES), f32)] * 2
        + [v((ny, EDGE, cap), f32)] * 2
        + [v((ny, cap, LANES), f32)] * 2
        + edge_bufs(4)
        + edge_bufs(1)
        + [v((slots, land), bf16), v((land, slots), bf16)]
        + [v((land, slots), bf16), v((slots, land), bf16)]
        + [dma((10,)), dma((4,))]
        + [dma((peers,))] * 6
        + [dma((8,))] * 4,
        compiler_params=pltpu.CompilerParams(collective_id=0, has_side_effects=True),
    )(
        depth, bed, east, south, rough, wet, soil[0], rain[0],
        column.reshape(1, land), block,
    )
    return out[0], out[1], out[2], out[3][None]


def solution(mesh):
    grid = P("gx", "gy")
    blocks = P("gx", "gy", None)
    return jax.shard_map(
        local, mesh=mesh,
        in_specs=(grid,) * 6 + (blocks,) * 3 + (grid,),
        out_specs=(grid,) * 3 + (blocks,),
        check_vma=False,
    )
```

time: 97.4 us -> 33 us (0.34)
  waiting for transfers between devices: 45.4 us -> 0 us
  Pallas kernels: 0 us -> 27.6 us
  between operations: 14.4 us -> 0.65 us
  other arithmetic: 11.5 us -> 0 us
  blocking collectives: 10.8 us -> 0 us
  starting transfers between devices: 10.2 us -> 0 us
    reduce_scatter x1 -> x0, waiting for transfers between devices: 28.1 us -> none  [local(): lax.psum_scatter(jax.ops.segment_sum(runoff, segment, num_segments=count...]
    pallas_call x0 -> x1, Pallas kernels: none -> 27.6 us  [local(): pl.pallas_call(functools.partial(kernel, nx, ny, cap), out_shape=[shape((...]
    ppermute x4 -> x0, waiting for transfers between devices: 17.3 us -> none  [the longest x2 12.3 us: padded_2(): lax.ppermute(head, axis, [((i + 1) % count, i) for i in range(ends)])]
    all_gather x1 -> x0, blocking collectives: 10.8 us -> none  [local(): piece = lax.all_gather(level_blocks, 'gy', axis=0, tiled=True)]
    ppermute x4 -> x0, starting transfers between devices: 10.2 us -> none  [the longest x2 6.99 us: padded_2(): lax.ppermute(tail, axis, [(i, (i + 1) % count) for i in range(ends)])]
    select_n x9 -> x0, other arithmetic: 5.45 us -> none  [the longest x8 4.73 us: face_flow(): return jnp.where(is_open, (previous - driving) / damping, 0.0)]
    unnamed x25 -> x10, local copies, waits for them, and re-layouts: 0.1 us -> 4.33 us
    add x6 -> x0, other arithmetic: 2.57 us -> none  [the longest x4 0.91 us: advance(): surface = bottom + height]
  transfers between devices with their start and end apart: 5 -> 0, of which waited for: 4 -> 0; matrix products, arithmetic and copies ran while one was open for 0% -> 0% of each run, Pallas kernels for 0% -> 0%
where the time goes in v1:
time: 33 us; the launch traced here: 32.5 us
  Pallas kernels  27.6 us (84%)
  local copies, waits for them, and re-layouts  4.33 us (13%)
  between operations  0.65 us (2%)
    pallas_call x1, Pallas kernels, local(): pl.pallas_call(functools.partial(kernel, nx, ny, cap), out_shape=[shape((...  27.6 us
    unnamed x10, local copies, waits for them, and re-layouts  4.33 us

profile of v1, /device:TPU:1, one launch (start us, length us, event | category | flops | bytes accessed | tf_op | source)
XLA Modules:
  0.0 32.5 jit_solution(7164528503411328250)
XLA Ops:
  0.6 27.6 %shard_map.129 = (f32[128,384]{1,0:T(8,128)}, f32[128,384]{1,0:T(8,128)}, f32[128,384]{1,0:T(8,128)}, f32[384,128]{1,0:T(8,128)}) custom-call(f32[128,384]{1,0:T(8,128)} %depth_in.1, f32[128,384]{1,0:T(8,128)} %bed_in.1, f32[128,384]{1,0:T(8,128)} %east_in.1, f32[128,384]{1,0:T(8,128)} %south_in.1, s32[128,384]{1,0:T(8,128)} %rough_in.1, s32[128,384]{1,0:T(8,128)} %wet_in.1, ...), custom_call_target="tpu_custom_call" | custom-call | tf_op jit(solution)/shard_map/pallas_call | solution.py:366
  28.2 0.0 copy-start.2
  28.2 1.7 %copy.18 = f32[128,384]{1,0:T(8,128)} copy(f32[128,384]{1,0:T(8,128)} %get-tuple-element.16) | data formatting | bytes 393216
  29.9 0.0 copy-done.2
  29.9 0.0 copy-start.1
  29.9 0.7 %copy.19 = f32[128,384]{1,0:T(8,128)} copy(f32[128,384]{1,0:T(8,128)S(1)} %copy-done.2) | data formatting | bytes 393216
  30.6 0.3 copy-done.1
  30.9 0.0 copy-start
  30.9 0.7 %copy.20 = f32[128,384]{1,0:T(8,128)} copy(f32[128,384]{1,0:T(8,128)S(1)} %copy-done.1) | data formatting | bytes 393216
  31.5 0.3 copy-done
  31.9 0.7 %copy.21 = f32[1,384,128]{2,1,0:T(8,128)} copy(f32[1,384,128]{2,1,0:T(8,128)S(1)} %bitcast.4) | data formatting | bytes 393216
Async XLA Ops:
  28.2 1.7 %copy-start.2 = (f32[128,384]{1,0:T(8,128)S(1)}, f32[128,384]{1,0:T(8,128)}, u32[]{:S(2)}) copy-start(f32[128,384]{1,0:T(8,128)} %get-tuple-element.17) | copy-start | bytes 589828
  29.9 1.0 %copy-start.1 = (f32[128,384]{1,0:T(8,128)S(1)}, f32[128,384]{1,0:T(8,128)}, u32[]{:S(2)}) copy-start(f32[128,384]{1,0:T(8,128)} %get-tuple-element.18) | copy-start | bytes 589828
  30.9 1.0 %copy-start = (f32[384,128]{1,0:T(8,128)S(1)}, f32[384,128]{1,0:T(8,128)}, u32[]{:S(2)}) copy-start(f32[384,128]{1,0:T(8,128)} %get-tuple-element.11) | copy-start | bytes 589828

commit v2 on v1

--- a/solution.py
+++ b/solution.py
@@ -53,14 +53,14 @@
 def kernel(
     nx, ny, cap,
     depth_in, bed_in, east_in, south_in, rough_in, wet_in, soil_in, rain_in, col_in, blk_in,
-    depth_out, east_out, south_out, soil_out,
-    h, bed, qe, qs, fric, rough, wet, soil, rain, col, blk, newsoil,
+    h, qe, qs, newsoil,
+    bed, fric, rough, wet, soil, rain, col, blk,
     base_e, base_s, coef_e, coef_s,
     give, take, give_idx, take_idx, give_lev, take_lev,
     st_rows, st_cols, st_in_rows, st_in_cols, st_in_corner,
     h_rows, h_cols, h_in_rows, h_in_cols, h_in_corner,
     place, place_t, where_to, where_to_t,
-    in_sem, out_sem, give_s, give_r, idx_s, idx_r, lev_s, lev_r, st_s, st_r, hs_s, hs_r,
+    in_sem, give_s, give_r, idx_s, idx_r, lev_s, lev_r, st_s, st_r, hs_s, hs_r,
 ):
     gx, gy = lax.axis_index("gx"), lax.axis_index("gy")
     tr, tc = rough.shape
@@ -311,12 +311,6 @@
             pltpu.roll(e, 1, 1) - e + pltpu.roll(s, 1, 0) - s
         )
 
-    stores = [
-        pltpu.make_async_copy(src.at[inner], dst, out_sem.at[i])
-        for i, (src, dst) in enumerate([(h, depth_out), (qe, east_out), (qs, south_out)])
-    ]
-    for c in stores:
-        c.start()
     blocks = jnp.concatenate(
         [h[0:tr, c * LANES : (c + 1) * LANES] for c in range(chunks)], axis=0
     )
@@ -332,15 +326,28 @@
     newsoil[...] = (
         store + rain[...] - runoff + INFIL_RATE * (1.0 - store) * (1.0 - jnp.exp(-mine))
     )
-    last = pltpu.make_async_copy(newsoil, soil_out, out_sem.at[3])
-    last.start()
     for c in sent:
         c.wait_send()
     st_done()
     h_done()
-    for c in stores:
+
+
+def write_out(h, qe, qs, newsoil, depth_out, east_out, south_out, soil_out, sem):
+    tr, tc = depth_out.shape
+    inner = (pl.ds(0, tr), pl.ds(0, tc))
+    copies = [
+        pltpu.make_async_copy(src, dst, sem.at[i])
+        for i, (src, dst) in enumerate(
+            [
+                (h.at[inner], depth_out), (qe.at[inner], east_out),
+                (qs.at[inner], south_out), (newsoil, soil_out),
+            ]
+        )
+    ]
+    for c in copies:
+        c.start()
+    for c in copies:
         c.wait()
-    last.wait()
 
 
 def local(depth, bed, east, south, rough, wet, soil, rain, column, block):
@@ -361,18 +368,18 @@
             v((2, k, EDGE, tc), f32), v((2, k, EDGE, tr), f32), v((4, k, EDGE, LANES), f32),
         ]
 
-    any_ = pl.BlockSpec(memory_space=pl.ANY)
+    any_ = pl.BlockSpec(memory_space=pltpu.MemorySpace.HBM)
+    vmem = pl.BlockSpec(memory_space=pltpu.VMEM)
     shape = jax.ShapeDtypeStruct
     out = pl.pallas_call(
         functools.partial(kernel, nx, ny, cap),
-        out_shape=[shape((tr, tc), f32)] * 3 + [shape((land, LANES), f32)],
+        out_shape=[shape(grid, f32)] * 3 + [shape((land, LANES), f32)],
         in_specs=[any_] * 10,
-        out_specs=[any_] * 4,
-        scratch_shapes=[v(grid, f32)] * 5
+        out_specs=[vmem] * 4,
+        scratch_shapes=[v(grid, f32)] * 2
         + [v((tr, tc), i32)] * 2
         + [v((land, LANES), f32)] * 2
         + [v((1, land), i32)] * 2
-        + [v((land, LANES), f32)]
         + [v(grid, f32)] * 4
         + [v((ny, cap, LANES), f32)] * 2
         + [v((ny, EDGE, cap), f32)] * 2
@@ -381,14 +388,23 @@
         + edge_bufs(1)
         + [v((slots, land), bf16), v((land, slots), bf16)]
         + [v((land, slots), bf16), v((slots, land), bf16)]
-        + [dma((10,)), dma((4,))]
+        + [dma((10,))]
         + [dma((peers,))] * 6
         + [dma((8,))] * 4,
-        compiler_params=pltpu.CompilerParams(collective_id=0, has_side_effects=True),
+        compiler_params=pltpu.CompilerParams(collective_id=0, has_side_effects=True, vmem_limit_bytes=24 << 20
+        ),
     )(
-        depth, bed, east, south, rough, wet, soil[0], rain[0],
-        column.reshape(1, land), block,
-    )
+        *[pltpu.with_memory_space_constraint(x, pltpu.MemorySpace.HBM) for x in (depth, bed, east, south, rough, wet, soil[0], rain[0],
+        column.reshape(1, land), block)]
+    )
+    out = pl.pallas_call(
+        write_out,
+        out_shape=[shape((tr, tc), f32)] * 3 + [shape((land, LANES), f32)],
+        in_specs=[vmem] * 4,
+        out_specs=[any_] * 4,
+        scratch_shapes=[dma((4,))],
+        compiler_params=pltpu.CompilerParams(vmem_limit_bytes=8 << 20),
+    )(*out)
     return out[0], out[1], out[2], out[3][None]
 
 

time: 33 us -> 28.9 us (0.88)
  local copies, waits for them, and re-layouts: 4.33 us -> 0 us
    unnamed x10 -> x0, local copies, waits for them, and re-layouts: 4.33 us -> none
    pallas_call x1 -> x2, Pallas kernels: 27.6 us -> 27.8 us  [the longest x1 26.9 us: local(): pl.pallas_call(functools.partial(kernel, nx, ny, cap), out_shape=[shape(g...]
where the time goes in v2:
time: 28.9 us; the launch traced here: 28.4 us
  Pallas kernels  27.8 us (96%)
  between operations  0.64 us (2%)
    pallas_call x1, Pallas kernels, local(): pl.pallas_call(functools.partial(kernel, nx, ny, cap), out_shape=[shape(g...  26.9 us
    pallas_call x1, Pallas kernels, local(): pl.pallas_call(write_out, out_shape=[shape((tr, tc), f32)] * 3 + [shape((...  0.91 us

profile of v2, /device:TPU:1, one launch (start us, length us, event | category | flops | bytes accessed | tf_op | source)
XLA Modules:
  0.0 28.4 jit_solution(5586618491423045980)
XLA Ops:
  0.6 26.9 %shard_map.129 = (f32[136,512]{1,0:T(8,128)S(1)}, f32[136,512]{1,0:T(8,128)S(1)}, f32[136,512]{1,0:T(8,128)S(1)}, f32[384,128]{1,0:T(8,128)S(1)}) custom-call(f32[128,384]{1,0:T(8,128)} %depth_in.1, f32[128,384]{1,0:T(8,128)} %bed_in.1, f32[128,384]{1,0:T(8,128)} %east_in.1, f32[128,384]{1,0:T(8,128)} %south_in.1, s32[128,384]{1,0:T(8,128)} %rough_in.1, ...), custom_call_target="tpu_custom_call" | custom-call | tf_op jit(solution)/shard_map/pallas_call | solution.py:374
  27.5 0.9 %shard_map.130 = (f32[128,384]{1,0:T(8,128)}, f32[128,384]{1,0:T(8,128)}, f32[128,384]{1,0:T(8,128)}, f32[384,128]{1,0:T(8,128)}) custom-call(f32[136,512]{1,0:T(8,128)S(1)} %get-tuple-element.12.h, f32[136,512]{1,0:T(8,128)S(1)} %get-tuple-element.13.qe, f32[136,512]{1,0:T(8,128)S(1)} %get-tuple-element.14.qs, f32[384,128]{1,0:T(8,128)S(1)} %get-tuple-element.15.newsoil), custom_call_target="tpu_custom_call" | custom-call | tf_op jit(solution)/shard_map/pallas_call | solution.py:400

commit v3 on v2

--- a/solution.py
+++ b/solution.py
@@ -30,8 +30,24 @@
 
 
 def pick(mask, x):
-    y = jnp.dot(mask, split3(x), preferred_element_type=jnp.float32)
+    x = x if x.dtype == jnp.bfloat16 else split3(x)
+    y = jnp.dot(mask, x, preferred_element_type=jnp.float32)
     return y[:, :LANES] + y[:, LANES : 2 * LANES] + y[:, 2 * LANES :]
+
+
+def flip(i, k, n):
+    if n & (n - 1):
+        return None
+    both, bit = 0, 1
+    while bit < n:
+        if k & bit:
+            both = both + bit * lax.rem(i // bit, 2)
+        bit *= 2
+    return i + k - 2 * both
+
+
+def offsets(n):
+    return sorted(range(1, n), key=lambda k: -bin(k).count("1"))
 
 
 def east_of(x):
@@ -159,32 +175,41 @@
 
     pl.semaphore_wait(barrier, total)
 
+    def to_peer(k):
+        peer = flip(gy, k, ny)
+        return lax.rem(gy + k, ny) if peer is None else peer
+
+    def from_peer(k):
+        peer = flip(gy, k, ny)
+        return lax.rem(gy + ny - k, ny) if peer is None else peer
+
+    def send(src, dst, ss, rs, k):
+        peer = to_peer(k)
+        c = pltpu.make_async_remote_copy(
+            src_ref=src.at[peer], dst_ref=dst.at[gy], send_sem=ss.at[k - 1],
+            recv_sem=rs.at[k - 1], device_id=(gx, peer), device_id_type=MESH,
+        )
+        c.start()
+        return c
+
     def to_all(src, dst, ss, rs):
-        out = []
-        for k in range(1, ny):
-            peer = lax.rem(gy + k, ny)
-            out.append(
-                pltpu.make_async_remote_copy(
-                    src_ref=src.at[peer], dst_ref=dst.at[gy], send_sem=ss.at[k - 1],
-                    recv_sem=rs.at[k - 1], device_id=(gx, peer), device_id_type=MESH,
-                )
-            )
-        for c in out:
-            c.start()
-        return out
+        return [send(src, dst, ss, rs, k) for k in offsets(ny)]
+
+    def receive(dst, src, ss, rs, k):
+        peer = from_peer(k)
+        pltpu.make_async_remote_copy(
+            src_ref=src.at[peer], dst_ref=dst.at[peer], send_sem=ss.at[k - 1],
+            recv_sem=rs.at[k - 1], device_id=(gx, peer), device_id_type=MESH,
+        ).wait_recv()
+        return peer
 
     def from_all(dst, src, ss, rs):
-        for k in range(1, ny):
-            peer = lax.rem(gy + ny - k, ny)
-            pltpu.make_async_remote_copy(
-                src_ref=src.at[peer], dst_ref=dst.at[peer], send_sem=ss.at[k - 1],
-                recv_sem=rs.at[k - 1], device_id=(gx, peer), device_id_type=MESH,
-            ).wait_recv()
+        for k in offsets(ny):
+            receive(dst, src, ss, rs, k)
 
     sent = to_all(give_idx, take_idx, idx_s, idx_r)
     sent += to_all(give, take, give_s, give_r)
     take_idx[pl.ds(gy, 1)] = give_idx[pl.ds(gy, 1)]
-    take[pl.ds(gy, 1)] = give[pl.ds(gy, 1)]
 
     for i in range(4, 9):
         loads[i].wait()
@@ -267,14 +292,15 @@
     )
     st_start()
 
-    place_t[...] = hit.T.astype(jnp.bfloat16)
+    for d in range(ny):
+        place_t[d] = hit[d * cap : (d + 1) * cap].T.astype(jnp.bfloat16)
 
     from_all(take_idx, give_idx, idx_s, idx_r)
-    ids = jnp.concatenate([take_idx[d] for d in range(ny)], axis=1)[0:1]
-    target = lax.broadcasted_iota(jnp.int32, (land, slots), 0).astype(jnp.float32) == ids
-    target = target.astype(jnp.float32)
-    where_to[...] = target.astype(jnp.bfloat16)
-    where_to_t[...] = target.T.astype(jnp.bfloat16)
+    for d in range(ny):
+        target = lax.broadcasted_iota(jnp.int32, (land, cap), 0).astype(jnp.float32)
+        target = (target == take_idx[d, 0:1]).astype(jnp.float32)
+        where_to[d] = target.astype(jnp.bfloat16)
+        where_to_t[d] = target.T.astype(jnp.bfloat16)
 
     st_wait()
     unstage(fixed, st_in_rows, st_in_cols, st_in_corner)
@@ -287,8 +313,10 @@
     coef_s[...] = jnp.where((fr > 0.0) & (f_s > 0.0), half * (fr + f_s), -1.0)
 
     loads[9].wait()
-    from_all(take, give, give_s, give_r)
-    inflow = pick(where_to[...], take[...].reshape(slots, LANES))
+    inflow = pick(where_to[gy], give[gy])
+    for k in offsets(ny):
+        peer = receive(take, give, give_s, give_r, k)
+        inflow = inflow + pick(where_to[peer], take[peer])
     for c in range(chunks):
         at = (pl.ds(0, tr), pl.ds(c * LANES, LANES))
         h[at] = h[at] + inflow[c * tr : (c + 1) * tr]
@@ -314,13 +342,15 @@
     blocks = jnp.concatenate(
         [h[0:tr, c * LANES : (c + 1) * LANES] for c in range(chunks)], axis=0
     )
-    levels = pick(where_to_t[...], blocks)
-    for d in range(ny):
-        give_lev[d] = levels[d * cap : (d + 1) * cap]
-    sent += to_all(give_lev, take_lev, lev_s, lev_r)
-    take_lev[pl.ds(gy, 1)] = give_lev[pl.ds(gy, 1)]
-    from_all(take_lev, give_lev, lev_s, lev_r)
-    mine = pick(place_t[...], take_lev[...].reshape(slots, LANES))
+    blocks = split3(blocks)
+    for k in offsets(ny):
+        peer = to_peer(k)
+        give_lev[peer] = pick(where_to_t[peer], blocks)
+        sent.append(send(give_lev, take_lev, lev_s, lev_r, k))
+    mine = pick(place_t[gy], pick(where_to_t[gy], blocks))
+    for k in offsets(ny):
+        peer = receive(take_lev, give_lev, lev_s, lev_r, k)
+        mine = mine + pick(place_t[peer], take_lev[peer])
     store = soil[...]
     runoff = rain[...] * store * store
     newsoil[...] = (
@@ -386,16 +416,21 @@
         + [v((ny, cap, LANES), f32)] * 2
         + edge_bufs(4)
         + edge_bufs(1)
-        + [v((slots, land), bf16), v((land, slots), bf16)]
-        + [v((land, slots), bf16), v((slots, land), bf16)]
+        + [v((slots, land), bf16), v((ny, land, cap), bf16)]
+        + [v((ny, land, cap), bf16), v((ny, cap, land), bf16)]
         + [dma((10,))]
         + [dma((peers,))] * 6
         + [dma((8,))] * 4,
         compiler_params=pltpu.CompilerParams(collective_id=0, has_side_effects=True, vmem_limit_bytes=24 << 20
         ),
     )(
-        *[pltpu.with_memory_space_constraint(x, pltpu.MemorySpace.HBM) for x in (depth, bed, east, south, rough, wet, soil[0], rain[0],
-        column.reshape(1, land), block)]
+        *(
+            pltpu.with_memory_space_constraint(x, pltpu.MemorySpace.HBM)
+            for x in (
+                depth, bed, east, south, rough, wet, soil[0], rain[0],
+                column.reshape(1, land), block,
+            )
+        )
     )
     out = pl.pallas_call(
         write_out,

time: 28.9 us -> 29.2 us (1.010)
  Pallas kernels: 27.8 us -> 28.3 us
    pallas_call x1, Pallas kernels: 26.9 us -> 27.4 us  [local(): pl.pallas_call(functools.partial(kernel, nx, ny, cap), out_shape=[shape(g...]
where the time goes in v3:
time: 29.2 us; the launch traced here: 28.9 us
  Pallas kernels  28.3 us (97%)
  between operations  0.64 us (2%)
    pallas_call x1, Pallas kernels, local(): pl.pallas_call(functools.partial(kernel, nx, ny, cap), out_shape=[shape(g...  27.4 us
    pallas_call x1, Pallas kernels, local(): pl.pallas_call(write_out, out_shape=[shape((tr, tc), f32)] * 3 + [shape((...  0.91 us

profile of v3, /device:TPU:1, one launch (start us, length us, event | category | flops | bytes accessed | tf_op | source)
XLA Modules:
  0.0 28.9 jit_solution(2304541909373111961)
XLA Ops:
  0.6 27.4 %shard_map.129 = (f32[136,512]{1,0:T(8,128)S(1)}, f32[136,512]{1,0:T(8,128)S(1)}, f32[136,512]{1,0:T(8,128)S(1)}, f32[384,128]{1,0:T(8,128)S(1)}) custom-call(f32[128,384]{1,0:T(8,128)} %depth_in.1, f32[128,384]{1,0:T(8,128)} %bed_in.1, f32[128,384]{1,0:T(8,128)} %east_in.1, f32[128,384]{1,0:T(8,128)} %south_in.1, s32[128,384]{1,0:T(8,128)} %rough_in.1, ...), custom_call_target="tpu_custom_call" | custom-call | tf_op jit(solution)/shard_map/pallas_call | solution.py:404
  28.0 0.9 %shard_map.130 = (f32[128,384]{1,0:T(8,128)}, f32[128,384]{1,0:T(8,128)}, f32[128,384]{1,0:T(8,128)}, f32[384,128]{1,0:T(8,128)}) custom-call(f32[136,512]{1,0:T(8,128)S(1)} %get-tuple-element.12.h, f32[136,512]{1,0:T(8,128)S(1)} %get-tuple-element.13.qe, f32[136,512]{1,0:T(8,128)S(1)} %get-tuple-element.14.qs, f32[384,128]{1,0:T(8,128)S(1)} %get-tuple-element.15.newsoil), custom_call_target="tpu_custom_call" | custom-call | tf_op jit(solution)/shard_map/pallas_call | solution.py:435

commit v4 on v3

--- a/solution.py
+++ b/solution.py
@@ -47,7 +47,7 @@
 
 
 def offsets(n):
-    return sorted(range(1, n), key=lambda k: -bin(k).count("1"))
+    return sorted(range(1, n), key=lambda k: bin(k).count("1"))
 
 
 def east_of(x):
@@ -302,6 +302,21 @@
         where_to[d] = target.astype(jnp.bfloat16)
         where_to_t[d] = target.T.astype(jnp.bfloat16)
 
+    loads[9].wait()
+    inflow = pick(where_to[gy], give[gy])
+    for k in offsets(ny):
+        peer = receive(take, give, give_s, give_r, k)
+        inflow = inflow + pick(where_to[peer], take[peer])
+    for c in range(chunks):
+        at = (pl.ds(0, tr), pl.ds(c * LANES, LANES))
+        h[at] = h[at] + inflow[c * tr : (c + 1) * tr]
+
+    stage((h,), h_rows, h_cols)
+    h_start, h_wait, h_done = edges(
+        h_rows, h_cols, h_in_rows, h_in_cols, h_in_corner, hs_s, hs_r
+    )
+    h_start()
+
     st_wait()
     unstage(fixed, st_in_rows, st_in_cols, st_in_corner)
     b, fr = bed[...], fric[...]
@@ -312,20 +327,6 @@
     coef_e[...] = jnp.where((fr > 0.0) & (f_e > 0.0), half * (fr + f_e), -1.0)
     coef_s[...] = jnp.where((fr > 0.0) & (f_s > 0.0), half * (fr + f_s), -1.0)
 
-    loads[9].wait()
-    inflow = pick(where_to[gy], give[gy])
-    for k in offsets(ny):
-        peer = receive(take, give, give_s, give_r, k)
-        inflow = inflow + pick(where_to[peer], take[peer])
-    for c in range(chunks):
-        at = (pl.ds(0, tr), pl.ds(c * LANES, LANES))
-        h[at] = h[at] + inflow[c * tr : (c + 1) * tr]
-
-    stage((h,), h_rows, h_cols)
-    h_start, h_wait, h_done = edges(
-        h_rows, h_cols, h_in_rows, h_in_cols, h_in_corner, hs_s, hs_r
-    )
-    h_start()
     h_wait()
     unstage((h,), h_in_rows, h_in_cols, h_in_corner)
 

time: 29.2 us -> 26.5 us (0.908)
  Pallas kernels: 28.3 us -> 25.7 us
    pallas_call x1, Pallas kernels: 27.4 us -> 24.8 us  [local(): pl.pallas_call(functools.partial(kernel, nx, ny, cap), out_shape=[shape(g...]
where the time goes in v4:
time: 26.5 us; the launch traced here: 26.4 us
  Pallas kernels  25.7 us (97%)
  between operations  0.64 us (2%)
    pallas_call x1, Pallas kernels, local(): pl.pallas_call(functools.partial(kernel, nx, ny, cap), out_shape=[shape(g...  24.8 us
    pallas_call x1, Pallas kernels, local(): pl.pallas_call(write_out, out_shape=[shape((tr, tc), f32)] * 3 + [shape((...  0.91 us

profile of v4, /device:TPU:1, one launch (start us, length us, event | category | flops | bytes accessed | tf_op | source)
XLA Modules:
  0.0 26.4 jit_solution(11029048141646315569)
XLA Ops:
  0.6 24.8 %shard_map.129 = (f32[136,512]{1,0:T(8,128)S(1)}, f32[136,512]{1,0:T(8,128)S(1)}, f32[136,512]{1,0:T(8,128)S(1)}, f32[384,128]{1,0:T(8,128)S(1)}) custom-call(f32[128,384]{1,0:T(8,128)} %depth_in.1, f32[128,384]{1,0:T(8,128)} %bed_in.1, f32[128,384]{1,0:T(8,128)} %east_in.1, f32[128,384]{1,0:T(8,128)} %south_in.1, s32[128,384]{1,0:T(8,128)} %rough_in.1, ...), custom_call_target="tpu_custom_call" | custom-call | tf_op jit(solution)/shard_map/pallas_call | solution.py:405
  25.5 0.9 %shard_map.130 = (f32[128,384]{1,0:T(8,128)}, f32[128,384]{1,0:T(8,128)}, f32[128,384]{1,0:T(8,128)}, f32[384,128]{1,0:T(8,128)}) custom-call(f32[136,512]{1,0:T(8,128)S(1)} %get-tuple-element.12.h, f32[136,512]{1,0:T(8,128)S(1)} %get-tuple-element.13.qe, f32[136,512]{1,0:T(8,128)S(1)} %get-tuple-element.14.qs, f32[384,128]{1,0:T(8,128)S(1)} %get-tuple-element.15.newsoil), custom_call_target="tpu_custom_call" | custom-call | tf_op jit(solution)/shard_map/pallas_call | solution.py:436

commit v5 on v4

--- a/solution.py
+++ b/solution.py
@@ -290,7 +290,6 @@
     st_start, st_wait, st_done = edges(
         st_rows, st_cols, st_in_rows, st_in_cols, st_in_corner, st_s, st_r
     )
-    st_start()
 
     for d in range(ny):
         place_t[d] = hit[d * cap : (d + 1) * cap].T.astype(jnp.bfloat16)
@@ -302,6 +301,7 @@
         where_to[d] = target.astype(jnp.bfloat16)
         where_to_t[d] = target.T.astype(jnp.bfloat16)
 
+    st_start()
     loads[9].wait()
     inflow = pick(where_to[gy], give[gy])
     for k in offsets(ny):

time: 26.5 us -> 26.3 us (level)
  Pallas kernels: 25.7 us -> 25.4 us
    pallas_call x1, Pallas kernels: 24.8 us -> 24.5 us  [local(): pl.pallas_call(functools.partial(kernel, nx, ny, cap), out_shape=[shape(g...]
where the time goes in v5:
time: 26.3 us; the launch traced here: 26 us
  Pallas kernels  25.4 us (97%)
  between operations  0.64 us (2%)
    pallas_call x1, Pallas kernels, local(): pl.pallas_call(functools.partial(kernel, nx, ny, cap), out_shape=[shape(g...  24.5 us
    pallas_call x1, Pallas kernels, local(): pl.pallas_call(write_out, out_shape=[shape((tr, tc), f32)] * 3 + [shape((...  0.91 us

profile of v5, /device:TPU:1, one launch (start us, length us, event | category | flops | bytes accessed | tf_op | source)
XLA Modules:
  0.0 26.0 jit_solution(2985234544180754102)
XLA Ops:
  0.6 24.5 %shard_map.129 = (f32[136,512]{1,0:T(8,128)S(1)}, f32[136,512]{1,0:T(8,128)S(1)}, f32[136,512]{1,0:T(8,128)S(1)}, f32[384,128]{1,0:T(8,128)S(1)}) custom-call(f32[128,384]{1,0:T(8,128)} %depth_in.1, f32[128,384]{1,0:T(8,128)} %bed_in.1, f32[128,384]{1,0:T(8,128)} %east_in.1, f32[128,384]{1,0:T(8,128)} %south_in.1, s32[128,384]{1,0:T(8,128)} %rough_in.1, ...), custom_call_target="tpu_custom_call" | custom-call | tf_op jit(solution)/shard_map/pallas_call | solution.py:405
  25.1 0.9 %shard_map.130 = (f32[128,384]{1,0:T(8,128)}, f32[128,384]{1,0:T(8,128)}, f32[128,384]{1,0:T(8,128)}, f32[384,128]{1,0:T(8,128)}) custom-call(f32[136,512]{1,0:T(8,128)S(1)} %get-tuple-element.12.h, f32[136,512]{1,0:T(8,128)S(1)} %get-tuple-element.13.qe, f32[136,512]{1,0:T(8,128)S(1)} %get-tuple-element.14.qs, f32[384,128]{1,0:T(8,128)S(1)} %get-tuple-element.15.newsoil), custom_call_target="tpu_custom_call" | custom-call | tf_op jit(solution)/shard_map/pallas_call | solution.py:436
